TPU v7x, 256 devices: a whole 4x4x8 slice. The times are simulated.
256 devices in a mesh: pair: 64 (over y, z, core), aux: 4 (over x).
Axes of the slice: x: 4, y: 4, z: 8, core: 2. Of those that a mesh axis runs over, the one named last changes fastest.
Arguments:
- factors: bfloat16 [64, 8192, 8, 128], P('pair', 'aux'), may hold values from -0.0625 to 0.0625
- amplitudes: bfloat16 [3072, 128, 128], P('pair'), may hold values from -6 to 6
- block_list: int32 [3072, 3], P('pair'), may hold values from 0 to 63, as said below
- owner_map: int32 [64], replicated, may hold values from 0 to 63, as said below
Outputs:
- residual_blocks: bfloat16 [3072, 128, 128], P('pair')
Inputs may be any that keep to these rules, and one draw needn't show every extreme that they name: `block_list`: each row (k, A, C) names an occupied orbital below 64 and two virtual blocks below 8; no row repeats. Among the 48 rows of one device at most 2 have orbitals with the same owner_map entry, and exactly 2 for some entry on every device. `owner_map`: A permutation: entry k is the row of factors that holds orbital k.
All inputs are finite; a program needn't handle non-finite values.
Results may differ from a plain program's by a relative error of at most 0.0046.
Values may be sent and summed in bfloat16 or wider, within the bound.
A program may use at most 64 MiB of HBM per device.

v0:
```python
import jax
import jax.numpy as jnp
from jax import lax
from jax.sharding import PartitionSpec as P

CAP = 2


def on_device(factors, amplitudes, block_list, owner_map):
    pair_count = lax.axis_size("pair")
    slot_total = pair_count * CAP
    block_count = amplitudes.shape[0]
    block_width = amplitudes.shape[1]
    virt_blocks = factors.shape[2]
    share_rows = factors.shape[1]
    orbital_total = owner_map.shape[0]
    orbitals = block_list[:, 0]
    block_a = block_list[:, 1]
    block_c = block_list[:, 2]
    matches = orbitals[:, None] == lax.iota(jnp.int32, orbital_total)[None, :]
    owners = jnp.sum(jnp.where(matches, owner_map[None, :], 0), axis=1)
    owner_hits = (owners[:, None] == lax.iota(jnp.int32, pair_count)[None, :]).astype(jnp.int32)
    earlier = jnp.cumsum(owner_hits, axis=0) - owner_hits
    slot_rank = jnp.sum(earlier * owner_hits, axis=1)
    slots = owners * CAP + slot_rank
    placing = slots[:, None] == lax.iota(jnp.int32, slot_total)[None, :]
    place_matrix = placing.astype(jnp.bfloat16)
    flat_blocks = amplitudes.reshape(block_count, block_width * block_width)
    send_blocks = jnp.einsum(
        "js,jm->sm", place_matrix, flat_blocks, preferred_element_type=jnp.float32
    )
    send_blocks = send_blocks.astype(jnp.bfloat16).reshape(
        pair_count, CAP, block_width, block_width
    )
    send_a = jnp.sum(jnp.where(placing, block_a[:, None] + 1, 0), axis=0)
    send_c = jnp.sum(jnp.where(placing, block_c[:, None] + 1, 0), axis=0)
    send_index = (
        jnp.stack([send_a, send_c], axis=-1).astype(jnp.bfloat16).reshape(pair_count, CAP, 2)
    )
    recv_blocks, recv_index = (
        lax.all_to_all(send_blocks, "pair", split_axis=0, concat_axis=0, tiled=True),
        lax.all_to_all(send_index, "pair", split_axis=0, concat_axis=0, tiled=True),
    )
    recv_index = recv_index.reshape(slot_total, 2).astype(jnp.int32) - 1
    slot_a = recv_index[:, 0]
    slot_c = recv_index[:, 1]
    onehot_a = (slot_a[:, None] == lax.iota(jnp.int32, virt_blocks)[None, :]).astype(jnp.bfloat16)
    onehot_c = (slot_c[:, None] == lax.iota(jnp.int32, virt_blocks)[None, :]).astype(jnp.bfloat16)
    combined = (onehot_c[:, :, None] * onehot_a[:, None, :]).reshape(
        slot_total, virt_blocks * virt_blocks
    )
    recv_flat = recv_blocks.reshape(slot_total, block_width * block_width)
    weights = jnp.einsum("sm,sn->mn", combined, recv_flat, preferred_element_type=jnp.float32)
    weights = weights.reshape(virt_blocks, virt_blocks, block_width, block_width)
    weights = jnp.transpose(weights, (0, 3, 1, 2)).reshape(
        virt_blocks * block_width, virt_blocks * block_width
    )
    weights = weights.astype(jnp.bfloat16)
    factor_flat = factors.reshape(share_rows, virt_blocks * block_width)
    factor_rows = factor_flat
    inter_share = lax.psum_scatter(
        jnp.dot(factor_rows, weights, preferred_element_type=jnp.float32),
        "pair",
        scatter_dimension=0,
        tiled=True,
    )
    inter_share = inter_share.astype(jnp.bfloat16)
    shard_rows = lax.all_gather(inter_share, "pair", axis=0, tiled=True)
    height = shard_rows.shape[0]
    factor_rows = factor_flat
    left = shard_rows.reshape(height, virt_blocks, block_width)
    right = factor_rows.reshape(height, virt_blocks, block_width)
    projected = jnp.einsum("qAa,qCc->ACac", left, right, preferred_element_type=jnp.float32)
    safe_a = jnp.maximum(slot_a, 0)
    safe_c = jnp.maximum(slot_c, 0)
    summed = lax.psum(projected, "aux")
    picked = summed[safe_a, safe_c].astype(jnp.bfloat16)
    picked = picked.reshape(pair_count, CAP, block_width, block_width)
    returned = lax.all_to_all(picked, "pair", split_axis=0, concat_axis=0, tiled=True)
    returned = returned.reshape(slot_total, block_width * block_width)
    result = jnp.einsum("js,sm->jm", place_matrix, returned, preferred_element_type=jnp.float32)
    return result.astype(jnp.bfloat16).reshape(block_count, block_width, block_width)


def solution(mesh):
    placed = (P("pair", "aux", None, None), P("pair", None, None), P("pair", None), P())
    return jax.shard_map(
        on_device, mesh=mesh, in_specs=placed, out_specs=P("pair", None, None), check_vma=False
    )
```

profile of v0, /device:TPU:1, one launch (start us, length us, event | category | flops | bytes accessed | tf_op | source)
XLA Modules:
  0.0 617.8 jit_solution(2545537378293932037)
XLA Ops:
  6.5 0.8 add_bitcast_fusion
  7.3 0.8 select_reduce_fusion.3
  8.2 0.1 fusion.18
  8.2 0.1 reduce_window_sum.11
  8.3 0.2 select_reduce_fusion.2
  8.5 0.1 select_reduce_fusion.1
  8.7 0.1 stack.10
  8.8 0.2 stack.9
  9.0 0.7 copy.26
  9.6 13.2 %all-to-all-start = ((bf16[64,2,2]{1,2,0:T(2,128)(2,1)}), bf16[64,2,2]{1,2,0:T(2,128)(2,1)S(1)}, u32[]{:S(2)}, u32[]{:S(2)}) async-start(bf16[64,2,2]{1,2,0:T(2,128)(2,1)} %copy.26), calls=%async_computation | async-start | bytes 65536 | tf_op jit(solution)/shard_map/all_to_all | solution.py:42
  22.8 2.8 fusion.10
  25.6 3.2 copy.39
  28.8 3.2 all-to-all-done
  32.0 7.3 %all-to-all-start.1 = ((bf16[64,2,128,128]{3,2,1,0:T(8,128)(2,1)}), bf16[64,2,128,128]{3,2,1,0:T(8,128)(2,1)}, u32[]{:S(2)}, u32[]{:S(2)}) async-start(bf16[64,2,128,128]{3,2,1,0:T(8,128)(2,1)} %bitcast.84), calls=%async_computation.1 | async-start | bytes 8388608 | tf_op jit(solution)/shard_map/all_to_all | solution.py:41
  39.3 0.2 reduce-scatter.4.cloned.1.call-start
  39.6 0.1 copy.27
  39.7 0.1 copy.28
  39.8 0.1 sub.11
  40.0 95.3 %all-to-all-done.1 = bf16[64,2,128,128]{3,2,1,0:T(8,128)(2,1)} async-done(((bf16[64,2,128,128]{3,2,1,0:T(8,128)(2,1)}), bf16[64,2,128,128]{3,2,1,0:T(8,128)(2,1)}, u32[]{:S(2)}, u32[]{:S(2)}) %all-to-all-start.1) | async-done | bytes 4194336 | tf_op jit(solution)/shard_map/all_to_all | solution.py:41
  135.2 7.7 %copy.70 = bf16[16,8,128,128]{3,1,2,0:T(8,128)(2,1)} copy(bf16[16,8,128,128]{3,2,1,0:T(8,128)(2,1)} %bitcast.39) | data formatting | bytes 8388608
  142.9 6.4 %copy.29 = bf16[128,16384]{0,1:T(8,128)(2,1)} copy(bf16[128,16384]{1,0:T(8,128)(2,1)} %bitcast.88) | data formatting | bytes 8388608 | tf_op jit(solution)/shard_map/reshape | solution.py:52
  149.3 3.8 convert_bitcast_fusion
  153.1 3.3 copy.30
  156.3 10.6 %convolution_bitcast_fusion = f32[2048,1024]{0,1:T(8,128)} fusion(bf16[256,8,8,128]{3,2,1,0:T(8,128)(2,1)} %bitcast.92, bf16[128,8,8,128]{3,2,1,0:T(8,128)(2,1)} %bitcast.90), kind=kOutput, calls=%fused_computation.3 | convolution fusion | flops 4294967296 | bytes 14680064 | tf_op jit(solution)/shard_map/dot_general | solution.py:62
  166.9 9.3 %copy.36 = f32[2048,1024]{1,0:T(8,128)} copy(f32[2048,1024]{0,1:T(8,128)} %convolution_bitcast_fusion) | data formatting | bytes 16777216
  176.2 0.0 reduce-scatter.4.cloned.1.call-update
  176.2 0.3 all-gather.2.cloned.1.call-start
  176.5 143.6 %reduce-scatter.4.cloned.1.call-done = f32[32,1024]{1,0:T(8,128)} async-done(((f32[2048,1024]{1,0:T(8,128)}), f32[32,1024]{1,0:T(8,128)}) %reduce-scatter.4.cloned.1.call-update) | async-done | bytes 131088 | tf_op jit(solution)/shard_map/reduce_scatter | solution.py:61
  320.2 1.5 convert_element_type.57
  321.7 0.0 all-gather.2.cloned.1.call-update
  321.7 83.6 %all-gather.2.cloned.1.call-done = bf16[2048,1024]{1,0:T(8,128)(2,1)} async-done(((bf16[32,1024]{1,0:T(8,128)(2,1)}), bf16[2048,1024]{1,0:T(8,128)(2,1)}) %all-gather.2.cloned.1.call-update) | async-done | bytes 4194320 | tf_op jit(solution)/shard_map/all_gather | solution.py:68
  405.3 6.5 %copy.32 = bf16[2048,1024]{0,1:T(8,128)(2,1)} copy(bf16[2048,1024]{1,0:T(8,128)(2,1)} %all-gather.2.cloned.1.call-done) | data formatting | bytes 8388608 | tf_op jit(solution)/shard_map/all_gather | solution.py:68
  411.8 9.9 %fusion.7 = f32[8,8,128,128]{3,2,1,0:T(8,128)} fusion(bf16[2048,8,128,1]{0,2,3,1:T(8,128)(2,1)} %bitcast.89, bf16[2048,8,128]{2,1,0:T(8,128)(2,1)} %bitcast.93), kind=kOutput, calls=%fused_computation.12 | convolution fusion | flops 4294967296 | bytes 12582912 | tf_op jit(solution)/shard_map/qAa,qCc->ACac/dot_general | solution.py:73
  421.7 78.1 %all-reduce.1 = bf16[8,8,128,128]{3,2,1,0:T(8,128)(2,1)S(1)} all-reduce(f32[8,8,128,128]{3,2,1,0:T(8,128)} %fusion.7), channel_id=1, replica_groups=mesh['pair'=64,'aux'=4] {'aux'}, use_global_device_ids=true, to_apply=%region_6.7 | all-reduce | flops 1048576 | bytes 6291456 | tf_op jit(solution)/shard_map/psum | solution.py:76
  499.8 3.1 gather_fusion
  502.8 103.9 %all_to_all.15 = bf16[64,2,128,128]{3,2,1,0:T(8,128)(2,1)S(1)} all-to-all(bf16[64,2,128,128]{3,2,1,0:T(8,128)(2,1)} %bitcast.86), channel_id=1, replica_groups=mesh['pair'=64,'aux'=4] {'pair'}, dimensions={0} | all-to-all | bytes 8388608 | tf_op jit(solution)/shard_map/all_to_all | solution.py:79
  606.7 2.7 fusion.15
  609.4 1.6 copy.44
  (7 shorter events, 0.1 us)
Async XLA Ops:
  9.6 22.4 %all-to-all-start = ((bf16[64,2,2]{1,2,0:T(2,128)(2,1)}), bf16[64,2,2]{1,2,0:T(2,128)(2,1)S(1)}, u32[]{:S(2)}, u32[]{:S(2)}) async-start(bf16[64,2,2]{1,2,0:T(2,128)(2,1)} %copy.26), calls=%async_computation | async-start | bytes 65536 | tf_op jit(solution)/shard_map/all_to_all | solution.py:42
  32.0 103.2 %all-to-all-start.1 = ((bf16[64,2,128,128]{3,2,1,0:T(8,128)(2,1)}), bf16[64,2,128,128]{3,2,1,0:T(8,128)(2,1)}, u32[]{:S(2)}, u32[]{:S(2)}) async-start(bf16[64,2,128,128]{3,2,1,0:T(8,128)(2,1)} %bitcast.84), calls=%async_computation.1 | async-start | bytes 8388608 | tf_op jit(solution)/shard_map/all_to_all | solution.py:41
  39.3 280.8 %reduce-scatter.4.cloned.1.call-start = ((), (), s32[]{:S(2)}) async-start(), calls=%async_computation.5 | async-start | bytes 8519680 | tf_op jit(solution)/shard_map/reduce_scatter | solution.py:61
  176.2 229.1 %all-gather.2.cloned.1.call-start = ((), (), s32[]{:S(2)}) async-start(), calls=%async_computation.4 | async-start | bytes 4259840 | tf_op jit(solution)/shard_map/all_gather | solution.py:68
Sparse Core Ops, SparseCore 0:
  176.4 143.7 reduce-scatter.3
  323.3 81.9 all-gather.1
where the time goes:
time: 619 us; the launch traced here: 618 us
  waiting for transfers between devices  326 us (53%)
  blocking collectives  182 us (29%)
  local copies, waits for them, and re-layouts  42.2 us (7%)
  matrix products  29.8 us (5%)
  starting transfers between devices  21 us (3%)
  between operations  13.5 us (2%)
    reduce_scatter x1, waiting for transfers between devices, on_device(): lax.psum_scatter(jnp.dot(factor_rows, weights, preferred_element_type=jnp...  144 us
    all_to_all x1, blocking collectives, on_device(): lax.all_to_all(picked, 'pair', split_axis=0, concat_axis=0, tiled=True)  104 us
    all_to_all x1, waiting for transfers between devices, on_device(): lax.all_to_all(send_blocks, 'pair', split_axis=0, concat_axis=0, tiled=True)  95.3 us
    all_gather x1, waiting for transfers between devices, on_device(): shard_rows = lax.all_gather(inter_share, 'pair', axis=0, tiled=True)  83.6 us
    psum x1, blocking collectives, on_device(): summed = lax.psum(projected, 'aux')  78.1 us
    unnamed x4, local copies, waits for them, and re-layouts  21.7 us
    all_to_all x1, starting transfers between devices, on_device(): lax.all_to_all(send_index, 'pair', split_axis=0, concat_axis=0, tiled=True)  13.2 us
  transfers between devices with their start and end apart: 4, of which 4 were waited for; matrix products, arithmetic and copies ran while one was open for 1% of the time, Pallas kernels for 0%

commit v1 on v0

--- a/solution.py
+++ b/solution.py
@@ -4,6 +4,11 @@
 from jax.sharding import PartitionSpec as P
 
 CAP = 2
+
+
+def add_all(x, axis):
+    parts = lax.all_gather(x, axis)
+    return jnp.sum(parts, axis=0)
 
 
 def on_device(factors, amplitudes, block_list, owner_map):
@@ -73,7 +78,7 @@
     projected = jnp.einsum("qAa,qCc->ACac", left, right, preferred_element_type=jnp.float32)
     safe_a = jnp.maximum(slot_a, 0)
     safe_c = jnp.maximum(slot_c, 0)
-    summed = lax.psum(projected, "aux")
+    summed = add_all(projected, "aux")
     picked = summed[safe_a, safe_c].astype(jnp.bfloat16)
     picked = picked.reshape(pair_count, CAP, block_width, block_width)
     returned = lax.all_to_all(picked, "pair", split_axis=0, concat_axis=0, tiled=True)

time: 619 us -> 705 us (1.14)
  waiting for transfers between devices: 326 us -> 479 us
  blocking collectives: 182 us -> 107 us
  other arithmetic: 3.67 us -> 11.9 us
    all_gather x0 -> x1, waiting for transfers between devices: none -> 154 us  [add_all(): parts = lax.all_gather(x, axis)]
    psum x1 -> x0, blocking collectives: 78.1 us -> none  [on_device(): summed = lax.psum(projected, 'aux')]
    reduce_sum x0 -> x1, other arithmetic: none -> 8.19 us  [add_all(): return jnp.sum(parts, axis=0)]
  transfers between devices with their start and end apart: 4 -> 5, of which waited for: 4 -> 5; matrix products, arithmetic and copies ran while one was open for 1% -> 1% of each run, Pallas kernels for 0% -> 0%
where the time goes in v1:
time: 705 us; the launch traced here: 704 us
  waiting for transfers between devices  479 us (68%)
  blocking collectives  107 us (15%)
  local copies, waits for them, and re-layouts  42.2 us (6%)
  matrix products  29.7 us (4%)
  starting transfers between devices  21 us (3%)
  between operations  13.2 us (2%)
  other arithmetic  11.9 us (2%)
    all_gather x1, waiting for transfers between devices, add_all(): parts = lax.all_gather(x, axis)  154 us
    reduce_scatter x1, waiting for transfers between devices, on_device(): lax.psum_scatter(jnp.dot(factor_rows, weights, preferred_element_type=jnp...  144 us
    all_to_all x1, blocking collectives, on_device(): lax.all_to_all(picked, 'pair', split_axis=0, concat_axis=0, tiled=True)  107 us
    all_to_all x1, waiting for transfers between devices, on_device(): lax.all_to_all(send_blocks, 'pair', split_axis=0, concat_axis=0, tiled=True)  95.3 us
    all_gather x1, waiting for transfers between devices, on_device(): shard_rows = lax.all_gather(inter_share, 'pair', axis=0, tiled=True)  83.3 us
    unnamed x4, local copies, waits for them, and re-layouts  21.7 us
  transfers between devices with their start and end apart: 5, of which 5 were waited for; matrix products, arithmetic and copies ran while one was open for 1% of the time, Pallas kernels for 0%

profile of v1, /device:TPU:1, one launch (start us, length us, event | category | flops | bytes accessed | tf_op | source)
XLA Modules:
  0.0 704.3 jit_solution(2927502939980917065)
XLA Ops:
  6.5 0.8 add_bitcast_fusion
  7.3 0.8 select_reduce_fusion.3
  8.2 0.1 fusion.18
  8.2 0.1 reduce_window_sum.11
  8.3 0.2 select_reduce_fusion.2
  8.5 0.1 select_reduce_fusion.1
  8.7 0.1 stack.10
  8.8 0.2 stack.9
  9.0 0.7 copy.26
  9.6 13.2 %all-to-all-start = ((bf16[64,2,2]{1,2,0:T(2,128)(2,1)}), bf16[64,2,2]{1,2,0:T(2,128)(2,1)S(1)}, u32[]{:S(2)}, u32[]{:S(2)}) async-start(bf16[64,2,2]{1,2,0:T(2,128)(2,1)} %copy.26), calls=%async_computation | async-start | bytes 65536 | tf_op jit(solution)/shard_map/all_to_all | solution.py:47
  22.8 2.8 fusion.10
  25.6 3.2 copy.39
  28.8 3.2 all-to-all-done
  32.0 7.3 %all-to-all-start.1 = ((bf16[64,2,128,128]{3,2,1,0:T(8,128)(2,1)}), bf16[64,2,128,128]{3,2,1,0:T(8,128)(2,1)}, u32[]{:S(2)}, u32[]{:S(2)}) async-start(bf16[64,2,128,128]{3,2,1,0:T(8,128)(2,1)} %bitcast.86), calls=%async_computation.1 | async-start | bytes 8388608 | tf_op jit(solution)/shard_map/all_to_all | solution.py:46
  39.3 0.2 reduce-scatter.4.cloned.1.call-start
  39.6 0.1 copy.27
  39.7 0.1 copy.28
  39.8 0.1 sub.11
  40.0 95.3 %all-to-all-done.1 = bf16[64,2,128,128]{3,2,1,0:T(8,128)(2,1)} async-done(((bf16[64,2,128,128]{3,2,1,0:T(8,128)(2,1)}), bf16[64,2,128,128]{3,2,1,0:T(8,128)(2,1)}, u32[]{:S(2)}, u32[]{:S(2)}) %all-to-all-start.1) | async-done | bytes 4194336 | tf_op jit(solution)/shard_map/all_to_all | solution.py:46
  135.2 7.7 %copy.70 = bf16[16,8,128,128]{3,1,2,0:T(8,128)(2,1)} copy(bf16[16,8,128,128]{3,2,1,0:T(8,128)(2,1)} %bitcast.40) | data formatting | bytes 8388608
  142.9 6.4 copy.29
  149.3 3.8 convert_bitcast_fusion
  153.1 3.3 copy.30
  156.3 10.6 %convolution_bitcast_fusion = f32[2048,1024]{0,1:T(8,128)} fusion(bf16[256,8,8,128]{3,2,1,0:T(8,128)(2,1)} %bitcast.94, bf16[128,8,8,128]{3,2,1,0:T(8,128)(2,1)} %bitcast.92), kind=kOutput, calls=%fused_computation.3 | convolution fusion | flops 4294967296 | bytes 14680064 | tf_op jit(solution)/shard_map/dot_general | solution.py:67
  166.9 9.3 %copy.36 = f32[2048,1024]{1,0:T(8,128)} copy(f32[2048,1024]{0,1:T(8,128)} %convolution_bitcast_fusion) | data formatting | bytes 16777216
  176.2 0.0 reduce-scatter.4.cloned.1.call-update
  176.2 0.0 all-gather.4.cloned.1.call-start
  176.3 143.9 %reduce-scatter.4.cloned.1.call-done = f32[32,1024]{1,0:T(8,128)} async-done(((f32[2048,1024]{1,0:T(8,128)}), f32[32,1024]{1,0:T(8,128)}) %reduce-scatter.4.cloned.1.call-update) | async-done | bytes 131088 | tf_op jit(solution)/shard_map/reduce_scatter | solution.py:66
  320.2 1.5 convert_element_type.57
  321.7 0.0 all-gather.4.cloned.1.call-update
  321.7 0.3 all-gather.6.cloned.1.call-start
  322.0 83.3 %all-gather.4.cloned.1.call-done = bf16[2048,1024]{1,0:T(8,128)(2,1)} async-done(((bf16[32,1024]{1,0:T(8,128)(2,1)}), bf16[2048,1024]{1,0:T(8,128)(2,1)}) %all-gather.4.cloned.1.call-update) | async-done | bytes 4194320 | tf_op jit(solution)/shard_map/all_gather | solution.py:73
  405.3 6.5 copy.32
  411.8 9.9 %fusion.7 = f32[8,8,128,128]{3,2,1,0:T(8,128)} fusion(bf16[2048,8,128,1]{0,2,3,1:T(8,128)(2,1)} %bitcast.91, bf16[2048,8,128]{2,1,0:T(8,128)(2,1)} %bitcast.95), kind=kOutput, calls=%fused_computation.12 | convolution fusion | flops 4294967296 | bytes 12582912 | tf_op jit(solution)/shard_map/qAa,qCc->ACac/dot_general | solution.py:78
  421.7 0.0 all-gather.6.cloned.1.call-update
  421.7 153.6 %all-gather.6.cloned.1.call-done = f32[32,8,128,128]{3,2,1,0:T(8,128)} async-done(((f32[8,8,128,128]{3,2,1,0:T(8,128)}), f32[32,8,128,128]{3,2,1,0:T(8,128)}) %all-gather.6.cloned.1.call-update) | async-done | bytes 16777232 | tf_op jit(solution)/shard_map/all_gather | solution.py:10
  575.4 8.2 %reduce_sum.49 = bf16[8,8,128,128]{3,2,1,0:T(8,128)(2,1)S(1)} reduce(f32[4,8,8,128,128]{4,3,2,1,0:T(8,128)} %bitcast.85, f32[]{:T(128)} %constant.18.clone.1), dimensions={0}, to_apply=%region_6.7 | reduce | flops 3145728 | bytes 18874372 | tf_op jit(solution)/shard_map/reduce_sum | solution.py:11
  583.6 3.1 gather_fusion
  586.6 106.9 %all_to_all.15 = bf16[64,2,128,128]{3,2,1,0:T(8,128)(2,1)S(1)} all-to-all(bf16[64,2,128,128]{3,2,1,0:T(8,128)(2,1)} %bitcast.88), channel_id=1, replica_groups=mesh['pair'=64,'aux'=4] {'pair'}, dimensions={0} | all-to-all | bytes 8388608 | tf_op jit(solution)/shard_map/all_to_all | solution.py:84
  693.5 2.7 fusion.15
  696.2 1.6 copy.44
  (7 shorter events, 0.1 us)
Async XLA Ops:
  9.6 22.4 %all-to-all-start = ((bf16[64,2,2]{1,2,0:T(2,128)(2,1)}), bf16[64,2,2]{1,2,0:T(2,128)(2,1)S(1)}, u32[]{:S(2)}, u32[]{:S(2)}) async-start(bf16[64,2,2]{1,2,0:T(2,128)(2,1)} %copy.26), calls=%async_computation | async-start | bytes 65536 | tf_op jit(solution)/shard_map/all_to_all | solution.py:47
  32.0 103.2 %all-to-all-start.1 = ((bf16[64,2,128,128]{3,2,1,0:T(8,128)(2,1)}), bf16[64,2,128,128]{3,2,1,0:T(8,128)(2,1)}, u32[]{:S(2)}, u32[]{:S(2)}) async-start(bf16[64,2,128,128]{3,2,1,0:T(8,128)(2,1)} %bitcast.86), calls=%async_computation.1 | async-start | bytes 8388608 | tf_op jit(solution)/shard_map/all_to_all | solution.py:46
  39.3 280.8 %reduce-scatter.4.cloned.1.call-start = ((), (), s32[]{:S(2)}) async-start(), calls=%async_computation.6 | async-start | bytes 8519680 | tf_op jit(solution)/shard_map/reduce_scatter | solution.py:66
  176.2 229.1 %all-gather.4.cloned.1.call-start = ((), (), s32[]{:S(2)}) async-start(), calls=%async_computation.4 | async-start | bytes 4259840 | tf_op jit(solution)/shard_map/all_gather | solution.py:73
  321.7 253.6 %all-gather.6.cloned.1.call-start = ((), (), s32[]{:S(2)}) async-start(), calls=%async_computation.5 | async-start | bytes 20971520 | tf_op jit(solution)/shard_map/all_gather | solution.py:10
Sparse Core Ops, SparseCore 0:
  176.4 143.7 reduce-scatter.3
  323.3 81.9 all-gather.3
  421.8 153.4 all-gather.5
